TPU v7x, 32 devices: a whole 2x2x4 slice. The times are simulated.
32 devices in a mesh: ctx: 16 (over z, y, x), head: 2 (over core).
Axes of the slice: x: 2, y: 2, z: 4, core: 2. Of those that a mesh axis runs over, the one named last changes fastest.
Arguments:
- query_raw: bfloat16 [16384, 4096], P('ctx', 'head')
- key_raw: bfloat16 [16384, 1024], P('ctx', 'head')
- values: bfloat16 [16384, 1024], P('ctx', 'head'), may hold values from -6 to 6
- output_gradient: bfloat16 [16384, 4096], P('ctx', 'head'), may hold values from -6 to 6
- query_gain: float32 [4096], P('head'), may hold values from 0.5 to 3
- key_norm_gain: float32 [1024], P('head'), may hold values from 0.5 to 3
- block_docs: int32 [128], replicated, may hold values from 0 to 20, never falling along the last dimension, each value on 1 to 24 neighbouring positions
Outputs:
- attended: bfloat16 [16384, 4096], P('ctx', 'head')
- query_grad: bfloat16 [16384, 4096], P('ctx', 'head')
- key_raw_gradient: bfloat16 [16384, 1024], P('ctx', 'head')
- value_grad: bfloat16 [16384, 1024], P('ctx', 'head')
- query_gain_grad: float32 [4096], P('head')
- key_gain_grad: float32 [1024], P('head')
Inputs may be any that keep to these rules, and one draw needn't show every extreme that they name: `block_docs`: document numbers never fall from one block to the next; each document covers 1 to 24 consecutive mask blocks, and one covers exactly 24.
All inputs are finite; a program needn't handle non-finite values.
Results may differ from a plain program's by a relative error of at most 0.024.
The roundings to bfloat16 on the way count: a program that leaves them out, or rounds other values in their place, can miss the bound.
Values may be sent and summed in bfloat16 or wider, within the bound.
No kernel may reach another device: no remote copies, remote signals or barrier semaphores. Data moves between devices by JAX's collectives and lax.ppermute only.
A program may use at most 128 MiB of HBM per device.

v0:
```python
import jax
import jax.numpy as jnp
from jax import lax
from jax.sharding import PartitionSpec as P

QUERY_HEADS = 32
KEY_VALUE_HEADS = 8
HEAD_SIZE = 128
WINDOW_REACH = 512
BLOCK = 128


EPS = 1e-06
NEGATIVE = -1e30


def from_behind(array, axis, by):
    peers = lax.axis_size(axis)
    pairs = [(i, i + by) for i in range(peers) if 0 <= i + by < peers]
    return lax.ppermute(array, axis, pairs)


def rescale_each_row(floats, summed, gain, row_width):
    scale_rows = lax.rsqrt(summed / row_width + EPS)[:, None]
    unit_rows = floats * scale_rows
    return (scale_rows, unit_rows, (unit_rows * gain).astype(jnp.bfloat16))


def send_back(key_gradient_total, value_gradient_total, halo_rows):
    return from_behind(
        (
            key_gradient_total[halo_rows - WINDOW_REACH : halo_rows],
            value_gradient_total[halo_rows - WINDOW_REACH : halo_rows],
        ),
        "ctx",
        -1,
    )


def local(query_raw, key_raw, values, output_gradient, query_gain, key_norm_gain, block_docs):
    tok_rows = query_raw.shape[0]
    query_cols = query_raw.shape[1]
    key_cols = key_raw.shape[1]
    kv_heads = key_cols // HEAD_SIZE
    query_group_count = query_cols // key_cols
    stride_rows = min(512, WINDOW_REACH)
    softmax_scale = HEAD_SIZE ** (-0.5)
    query_float = query_raw.astype(jnp.float32)
    key_single_precision = key_raw.astype(jnp.float32)
    query_sq, key_squared = lax.psum(
        (
            jnp.sum(query_float * query_float, axis=1),
            jnp.sum(key_single_precision * key_single_precision, axis=1),
        ),
        "head",
    )
    query_scale, query_unit, query_normalized = rescale_each_row(
        query_float, query_sq, query_gain, QUERY_HEADS * HEAD_SIZE
    )
    key_inverse_scale, key_unit_rows, key_normalized = rescale_each_row(
        key_single_precision, key_squared, key_norm_gain, KEY_VALUE_HEADS * HEAD_SIZE
    )
    halo_keys, halo_values = from_behind((key_normalized, values), "ctx", 1)
    halo_rows = halo_keys.shape[0]
    ext_keys = jnp.concatenate([halo_keys, key_normalized])
    ext_values = jnp.concatenate([halo_values, values])
    first_block = lax.axis_index("ctx") * (tok_rows // BLOCK)
    doc_padded = jnp.concatenate([jnp.full((halo_rows // BLOCK,), -1, jnp.int32), block_docs])
    doc_ext = jnp.repeat(
        lax.dynamic_slice_in_dim(doc_padded, first_block, (halo_rows + tok_rows) // BLOCK, 0), BLOCK
    )
    doc_query = doc_ext[halo_rows:]
    key_total_count = stride_rows + WINDOW_REACH
    distance = (
        jnp.arange(stride_rows, dtype=jnp.int32)[:, None]
        + WINDOW_REACH
        - jnp.arange(key_total_count, dtype=jnp.int32)[None, :]
    )
    in_window = (distance >= 0) & (distance < WINDOW_REACH)

    def attend(running, block_index):
        key_gradient_total, value_gradient_total = running
        leading_row = block_index * stride_rows
        lowest = halo_rows - WINDOW_REACH + leading_row
        query_block = lax.dynamic_slice_in_dim(
            query_normalized, leading_row, stride_rows, 0
        ).reshape(stride_rows, kv_heads, query_group_count, HEAD_SIZE)
        gradient_block = lax.dynamic_slice_in_dim(
            output_gradient, leading_row, stride_rows, 0
        ).reshape(stride_rows, kv_heads, query_group_count, HEAD_SIZE)
        key_block = lax.dynamic_slice_in_dim(ext_keys, lowest, key_total_count, 0).reshape(
            key_total_count, kv_heads, HEAD_SIZE
        )
        value_block = lax.dynamic_slice_in_dim(ext_values, lowest, key_total_count, 0).reshape(
            key_total_count, kv_heads, HEAD_SIZE
        )
        doc_rows = lax.dynamic_slice_in_dim(doc_query, leading_row, stride_rows, 0)
        doc_keys = lax.dynamic_slice_in_dim(doc_ext, lowest, key_total_count, 0)
        visible = in_window & (doc_rows[:, None] == doc_keys[None, :])
        scores = (
            jnp.einsum("ighd,jgd->ghij", query_block, key_block, preferred_element_type=jnp.float32)
            * softmax_scale
        )
        row_max = jnp.max(jnp.where(visible, scores, NEGATIVE), axis=-1, keepdims=True)
        expo = jnp.where(visible, jnp.exp(scores - row_max), 0.0)
        weights = expo / jnp.sum(expo, axis=-1, keepdims=True)
        weights_low = weights.astype(jnp.bfloat16)
        out_blk = jnp.einsum(
            "ghij,jgd->ighd", weights_low, value_block, preferred_element_type=jnp.float32
        ).astype(jnp.bfloat16)
        delta = jnp.einsum(
            "ighd,ighd->ghi", gradient_block, out_blk, preferred_element_type=jnp.float32
        )
        dweights = jnp.einsum(
            "ighd,jgd->ghij", gradient_block, value_block, preferred_element_type=jnp.float32
        )
        dscores_low = (weights * (dweights - delta[..., None])).astype(jnp.bfloat16)
        dquery_blk = (
            jnp.einsum("ghij,jgd->ighd", dscores_low, key_block, preferred_element_type=jnp.float32)
            * softmax_scale
        )
        key_gradient_block = (
            jnp.einsum(
                "ghij,ighd->jgd", dscores_low, query_block, preferred_element_type=jnp.float32
            )
            * softmax_scale
        )
        value_gradient_block = jnp.einsum(
            "ghij,ighd->jgd", weights_low, gradient_block, preferred_element_type=jnp.float32
        )
        present_key = lax.dynamic_slice_in_dim(key_gradient_total, lowest, key_total_count, 0)
        key_gradient_total = lax.dynamic_update_slice_in_dim(
            key_gradient_total,
            present_key + key_gradient_block.reshape(key_total_count, key_cols),
            lowest,
            0,
        )
        present_value = lax.dynamic_slice_in_dim(value_gradient_total, lowest, key_total_count, 0)
        value_gradient_total = lax.dynamic_update_slice_in_dim(
            value_gradient_total,
            present_value + value_gradient_block.reshape(key_total_count, key_cols),
            lowest,
            0,
        )
        return (
            (key_gradient_total, value_gradient_total),
            (out_blk.reshape(stride_rows, query_cols), dquery_blk.reshape(stride_rows, query_cols)),
        )

    blank_start = jnp.zeros((halo_rows + tok_rows, key_cols), jnp.float32)
    total_blocks = tok_rows // stride_rows
    halo_blocks = WINDOW_REACH // stride_rows
    first_state, first_outs = lax.scan(
        attend, (blank_start, blank_start), jnp.arange(halo_blocks, dtype=jnp.int32)
    )
    back_key, back_value = send_back(first_state[0], first_state[1], halo_rows)
    (key_gradient_total, value_gradient_total), rest_outs = lax.scan(
        attend, first_state, jnp.arange(halo_blocks, total_blocks, dtype=jnp.int32)
    )
    out_blocks = jnp.concatenate([first_outs[0], rest_outs[0]])
    dquery_blocks = jnp.concatenate([first_outs[1], rest_outs[1]])
    attended = out_blocks.reshape(tok_rows, query_cols)
    dquery = dquery_blocks.reshape(tok_rows, query_cols)
    tail_start = tok_rows - WINDOW_REACH
    dkey_local = key_gradient_total[halo_rows:]
    dvalue_local = value_gradient_total[halo_rows:]
    dkey = jnp.concatenate([dkey_local[:tail_start], dkey_local[tail_start:] + back_key])
    value_grad = jnp.concatenate(
        [dvalue_local[:tail_start], dvalue_local[tail_start:] + back_value]
    ).astype(jnp.bfloat16)
    query_scaled = dquery * query_gain
    key_rescaled = dkey * key_norm_gain
    query_dot, key_product = lax.psum(
        (jnp.sum(query_scaled * query_unit, axis=1), jnp.sum(key_rescaled * key_unit_rows, axis=1)),
        "head",
    )
    query_grad = (
        query_scale * (query_scaled - query_unit * (query_dot / (QUERY_HEADS * HEAD_SIZE))[:, None])
    ).astype(jnp.bfloat16)
    key_raw_gradient = (
        key_inverse_scale
        * (key_rescaled - key_unit_rows * (key_product / (KEY_VALUE_HEADS * HEAD_SIZE))[:, None])
    ).astype(jnp.bfloat16)
    query_gain_grad, key_gain_grad = lax.psum(
        (jnp.sum(dquery * query_unit, axis=0), jnp.sum(dkey * key_unit_rows, axis=0)), "ctx"
    )
    return (attended, query_grad, key_raw_gradient, value_grad, query_gain_grad, key_gain_grad)


def solution(mesh):
    placed = (
        P("ctx", "head"),
        P("ctx", "head"),
        P("ctx", "head"),
        P("ctx", "head"),
        P("head"),
        P("head"),
        P(),
    )
    return jax.shard_map(
        local,
        mesh=mesh,
        in_specs=placed,
        out_specs=(
            P("ctx", "head"),
            P("ctx", "head"),
            P("ctx", "head"),
            P("ctx", "head"),
            P("head"),
            P("head"),
        ),
        check_vma=False,
    )
```

profile of v0, /device:TPU:0, one launch (start us, length us, event | category | flops | bytes accessed | tf_op | source)
XLA Modules:
  0.0 403.8 jit_solution(2112004690417707157)
XLA Ops:
  0.6 5.8 %collective-permute-start = (bf16[1024,512]{1,0:T(8,128)(2,1)}, bf16[1024,512]{1,0:T(8,128)(2,1)}, u32[]{:S(2)}, u32[]{:S(2)}) collective-permute-start(bf16[1024,512]{1,0:T(8,128)(2,1)} %param.9), channel_id=1, source_target_pairs={{0,2},{2,4},{4,6},{6,8},{8,10},{10,12},{12,14},{14,16},{16,18},{18... | collective-permute-start | bytes 3145736 | tf_op jit(solution)/shard_map/ppermute | solution.py:20
  6.5 1.5 copy.41
  8.2 6.5 %copy.42 = bf16[1024,2048]{0,1:T(8,128)(2,1)} copy(bf16[1024,2048]{1,0:T(8,128)(2,1)} %param.7) | data formatting | bytes 8388608 | tf_op args[0]
  14.8 3.2 fusion.32
  18.0 2.5 all-reduce.5
  20.8 3.9 collective-permute-start.1
  26.0 2.8 fusion.26
  28.8 1.6 fusion.63
  30.4 1.3 copy-done.13
  31.7 2.7 fusion.62
  34.4 3.9 copy.117
  38.3 3.9 copy.118
  42.4 2.0 compare_and_fusion.1
  44.4 19.6 %fusion.67 = (f32[4,4,512]{2,1,0:T(4,128)}, f32[4,4,512,1024]{2,3,1,0:T(8,128)}) fusion(pred[512,1024]{0,1:T(8,128)(4,1)} %get-tuple-element.101, bf16[1024,4,128,1]{0,2,3,1:T(8,128)(2,1)S(1)} %bitcast.170, bf16[512,4,4,128]{0,3,2,1:T(8,128)(2,1)S(1)} %bitcast.175), kind=kOutput, calls=%fused_computation.109 | convolution fusion | flops 4345299968 | bytes 37257216 | tf_op jit(solution)/shard_map/while/body/eval_jaxpr/sub | solution.py:105
  64.0 12.3 %fusion.21 = bf16[4,4,512,1024]{2,3,1,0:T(8,128)(2,1)S(1)} fusion(f32[4,4,512,1024]{2,3,1,0:T(8,128)} %get-tuple-element.107, f32[4,4,512]{2,1,0:T(4,128)} %get-tuple-element.106), kind=kLoop, calls=%fused_computation.29 | loop fusion | flops 16777216 | bytes 50364416 | tf_op jit(solution)/shard_map/while/body/eval_jaxpr/convert_element_type | solution.py:107
  76.3 8.3 %fusion.70 = f32[4,1024,128,1]{1,2,3,0:T(8,128)} fusion(bf16[4,4,512,1024]{2,3,1,0:T(8,128)(2,1)S(1)} %fusion.21, bf16[512,4,4,128]{0,3,2,1:T(8,128)(2,1)} %bitcast.162), kind=kOutput, calls=%fused_computation.112 | convolution fusion | flops 2147483648 | bytes 20971520 | tf_op jit(solution)/shard_map/while/body/eval_jaxpr/ghij,ighd->jgd/dot_general | solution.py:128
  84.6 6.4 %fusion.33 = (f32[4,4,512]{2,1,0:T(4,128)}, bf16[4,4,512,128]{2,3,1,0:T(8,128)(2,1)}) fusion(bf16[512,2048]{0,1:T(8,128)(2,1)} %copy.118, bf16[4,4,512,1024]{2,3,1,0:T(8,128)(2,1)S(1)} %fusion.21, bf16[1024,4,128,1]{2,1,0,3:T(4,128)(2,1)} %bitcast.183), kind=kOutput, calls=%fused_computation.46 | convolution fusion | flops 2152718336 | bytes 22052864 | tf_op jit(solution)/shard_map/while/body/eval_jaxpr/ghij,jgd->ighd/dot_general | solution.py:108
  91.0 31.4 %fusion.3 = bf16[4,4,512,1024]{2,3,1,0:T(8,128)(2,1)} fusion(f32[4,4,512]{2,1,0:T(4,128)} %get-tuple-element.110, f32[4,4,512,1024]{2,3,1,0:T(8,128)} %get-tuple-element.107, f32[4,4,512]{2,1,0:T(4,128)} %get-tuple-element.106, bf16[512,4,4,128]{0,3,2,1:T(8,128)(2,1)} %bitcast.163, bf16[1024,4,128,1]{2,1,0,3:T(4,128)(2,1)} %bitcast.184), kind=kOutput, calls=%fused_computation.4 | convolution fusion | flops 2181038080 | bytes 53542912 | tf_op jit(solution)/shard_map/while/body/eval_jaxpr/ighd,jgd->ghij/dot_general | solution.py:114
  122.4 13.3 %bitcast_multiply_fusion = f32[4,128,1024]{2,1,0:T(8,128)} fusion(bf16[512,4,4,128]{0,3,2,1:T(8,128)(2,1)} %bitcast.176, bf16[4,4,512,1024]{2,3,1,0:T(8,128)(2,1)} %fusion.3), kind=kOutput, calls=%fused_computation.67 | convolution fusion | flops 2148007936 | bytes 20971520 | tf_op jit(solution)/shard_map/while/body/eval_jaxpr/ghij,ighd->jgd/dot_general | solution.py:123
  135.7 1.8 copy.65
  137.5 10.3 %broadcast_multiply_fusion = f32[4,128,4,512]{3,1,2,0:T(8,128)} fusion(bf16[1024,4,128,1]{0,2,3,1:T(8,128)(2,1)S(1)} %bitcast.171, bf16[4,4,512,1024]{2,3,1,0:T(8,128)(2,1)} %fusion.3), kind=kOutput, calls=%fused_computation.69 | convolution fusion | flops 2148532224 | bytes 22020096 | tf_op jit(solution)/shard_map/while/body/eval_jaxpr/ghij,jgd->ighd/dot_general | solution.py:119
  147.9 2.2 pad_maximum_fusion.3
  150.1 2.3 copy.40
  152.4 2.1 pad_maximum_fusion.2
  154.5 19.3 %fusion.68 = (f32[4,4,512]{2,1,0:T(4,128)S(1)}, f32[4,4,512,1024]{2,3,1,0:T(8,128)}) fusion(pred[512,1024]{0,1:T(8,128)(4,1)} %get-tuple-element.100, bf16[1024,4,128,1]{0,2,3,1:T(8,128)(2,1)} %bitcast.181, bf16[512,4,4,128]{0,3,2,1:T(8,128)(2,1)S(1)} %bitcast.174), kind=kOutput, calls=%fused_computation.110 | convolution fusion | flops 4345299968 | bytes 37257216 | tf_op jit(solution)/shard_map/while/body/eval_jaxpr/sub | solution.py:105
  173.8 12.3 %fusion.20 = bf16[4,4,512,1024]{2,3,1,0:T(8,128)(2,1)S(1)} fusion(f32[4,4,512,1024]{2,3,1,0:T(8,128)} %get-tuple-element.109, f32[4,4,512]{2,1,0:T(4,128)S(1)} %get-tuple-element.108), kind=kLoop, calls=%fused_computation.28 | loop fusion | flops 16777216 | bytes 50364416 | tf_op jit(solution)/shard_map/while/body/eval_jaxpr/convert_element_type | solution.py:107
  186.1 8.4 %fusion.69 = f32[4,1024,128,1]{1,2,3,0:T(8,128)} fusion(bf16[4,4,512,1024]{2,3,1,0:T(8,128)(2,1)S(1)} %fusion.20, bf16[512,4,4,128]{0,3,2,1:T(8,128)(2,1)} %bitcast.160), kind=kOutput, calls=%fused_computation.111 | convolution fusion | flops 2147483648 | bytes 20971520 | tf_op jit(solution)/shard_map/while/body/eval_jaxpr/ghij,ighd->jgd/dot_general | solution.py:128
  194.5 6.1 %fusion.34 = (f32[4,4,512]{2,1,0:T(4,128)}, bf16[4,128,4,512]{3,1,2,0:T(8,128)(2,1)}) fusion(bf16[512,2048]{0,1:T(8,128)(2,1)} %copy.117, bf16[1024,4,128,1]{0,2,3,1:T(8,128)(2,1)S(1)} %bitcast.185, bf16[4,4,512,1024]{2,3,1,0:T(8,128)(2,1)S(1)} %fusion.20), kind=kOutput, calls=%fused_computation.48 | convolution fusion | flops 2152718336 | bytes 22052864 | tf_op jit(solution)/shard_map/while/body/eval_jaxpr/ghij,jgd->ighd/dot_general | solution.py:108
  200.5 17.5 %fusion.5 = bf16[4,4,512,1024]{2,3,1,0:T(8,128)(2,1)} fusion(f32[4,4,512]{2,1,0:T(4,128)} %get-tuple-element.112, f32[4,4,512,1024]{2,3,1,0:T(8,128)} %get-tuple-element.109, f32[4,4,512]{2,1,0:T(4,128)} %copy-done.23, bf16[1024,4,128,1]{0,2,3,1:T(8,128)(2,1)S(1)} %bitcast.186, bf16[512,4,4,128]{0,3,2,1:T(8,128)(2,1)} %bitcast.161), kind=kOutput, calls=%fused_computation.7 | convolution fusion | flops 2181038080 | bytes 53542912 | tf_op jit(solution)/shard_map/while/body/eval_jaxpr/ighd,jgd->ghij/dot_general | solution.py:114
  218.0 12.0 %bitcast_multiply_fusion.1 = f32[4,128,1024]{2,1,0:T(8,128)S(1)} fusion(bf16[512,4,4,128]{0,3,2,1:T(8,128)(2,1)} %bitcast.173, bf16[4,4,512,1024]{2,3,1,0:T(8,128)(2,1)} %fusion.5), kind=kOutput, calls=%fused_computation.68 | convolution fusion | flops 2148007936 | bytes 20971520 | tf_op jit(solution)/shard_map/while/body/eval_jaxpr/ghij,ighd->jgd/dot_general | solution.py:123
  230.0 8.3 %broadcast_multiply_fusion.1 = f32[4,128,4,512]{3,1,2,0:T(8,128)S(1)} fusion(bf16[1024,4,128,1]{0,2,3,1:T(8,128)(2,1)S(1)} %bitcast.182, bf16[4,4,512,1024]{2,3,1,0:T(8,128)(2,1)} %fusion.5), kind=kOutput, calls=%fused_computation.70 | convolution fusion | flops 2148532224 | bytes 22020096 | tf_op jit(solution)/shard_map/while/body/eval_jaxpr/ghij,jgd->ighd/dot_general | solution.py:119
  239.4 4.3 %copy.119 = f32[2,256,8,512]{3,2,0,1:T(8,128)} copy(f32[2,256,8,512]{3,2,1,0:T(8,128)S(1)} %maximum_bitcast_fusion) | data formatting | bytes 16777216 | tf_op jit(solution)/shard_map/reshape | solution.py:163
  244.7 2.3 pad_maximum_fusion
  247.0 6.2 %copy.50 = bf16[2,512,2048]{2,1,0:T(8,128)(2,1)} copy(bf16[2,512,2048]{1,2,0:T(8,128)(2,1)} %pad_maximum_fusion) | data formatting | bytes 8388608 | tf_op jit(solution)/shard_map/concatenate | solution.py:160
  254.5 1.3 copy.66
  258.4 2.9 copy.63
  261.3 2.3 fusion.47
  265.2 1.7 copy-done
  266.9 4.5 %fusion.31 = (f32[2048]{0:T(1024)S(1)}, f32[1024]{0:T(1024)S(1)}) fusion(f32[1024,2048]{0,1:T(8,128)} %bitcast.158, bf16[1024,2048]{0,1:T(8,128)(2,1)S(1)} %copy-done, f32[1024]{0:T(1024)S(1)} %copy-done.20, f32[2048]{0:T(1024)S(1)} %copy-done.18), kind=kLoop, calls=%fused_computation.41 | loop fusion | flops 14676992 | bytes 12607488 | tf_op jit(solution)/shard_map/reduce_sum | solution.py:185
  271.4 34.0 %collective-permute-done.2 = f32[512,512]{0,1:T(8,128)} collective-permute-done((f32[512,512]{0,1:T(8,128)}, f32[512,512]{0,1:T(8,128)}, u32[]{:S(2)}, u32[]{:S(2)}) %collective-permute-start.2) | collective-permute-done | bytes 1048608 | tf_op jit(solution)/shard_map/ppermute | solution.py:20
  305.4 1.6 fusion.64
  307.6 2.5 all-reduce.4
  310.1 7.1 %fusion.30 = bf16[1024,2048]{0,1:T(8,128)(2,1)} fusion(bf16[1024,2048]{0,1:T(8,128)(2,1)} %copy.42, f32[1024,2048]{0,1:T(8,128)} %bitcast.159, f32[1024]{0:T(1024)S(1)} %broadcast_multiply_fusion.2, f32[2048]{0:T(1024)S(1)} %copy-done.18, f32[1024]{0:T(1024)S(1)} %copy-done.20), kind=kLoop, calls=%fused_computation.40 | loop fusion | flops 14680064 | bytes 16793600 | tf_op jit(solution)/shard_map/convert_element_type | solution.py:179
  317.2 6.4 %copy.67 = bf16[1024,2048]{1,0:T(8,128)(2,1)} copy(bf16[1024,2048]{0,1:T(8,128)(2,1)} %fusion.30) | data formatting | bytes 8388608
  323.7 1.4 fusion.43
  325.1 2.3 copy.68
  327.4 73.3 %all-reduce.3 = (f32[2048]{0:T(1024)}, f32[512]{0:T(512)}) all-reduce(f32[2048]{0:T(1024)S(1)} %get-tuple-element.72, f32[512]{0:T(512)S(1)} %get-tuple-element.74), channel_id=1, replica_groups=mesh['ctx'=16,'head'=2] {'ctx'}, use_global_device_ids=true, to_apply=%region_13.14 | all-reduce | flops 2560 | bytes 20480 | tf_op jit(solution)/shard_map/psum | solution.py:184
  400.8 1.7 fusion.55
  (77 shorter events, 11.1 us)
Async XLA Ops:
  0.6 147.2 %collective-permute-start = (bf16[1024,512]{1,0:T(8,128)(2,1)}, bf16[1024,512]{1,0:T(8,128)(2,1)}, u32[]{:S(2)}, u32[]{:S(2)}) collective-permute-start(bf16[1024,512]{1,0:T(8,128)(2,1)} %param.9), channel_id=1, source_target_pairs={{0,2},{2,4},{4,6},{6,8},{8,10},{10,12},{12,14},{14,16},{16,18},{18... | collective-permute-start | bytes 3145736 | tf_op jit(solution)/shard_map/ppermute | solution.py:20
  8.0 12.5 %copy-start.1 = (bf16[1024,512]{0,1:T(8,128)(2,1)}, bf16[1024,512]{0,1:T(8,128)(2,1)S(1)}, u32[]{:S(2)}) copy-start(bf16[1024,512]{0,1:T(8,128)(2,1)S(1)} %copy.41) | copy-start | bytes 3145732
  14.7 5.7 %copy-start.24 = (f32[512]{0:T(512)S(1)}, f32[512]{0:T(512)}, u32[]{:S(2)}) copy-start(f32[512]{0:T(512)} %param.12) | copy-start | bytes 6148
  14.7 9.9 %copy-start.26 = (s32[128]{0:T(128)S(1)}, s32[128]{0:T(128)}, u32[]{:S(2)}) copy-start(s32[128]{0:T(128)} %param.13) | copy-start | bytes 1540
  14.7 10.1 %copy-start.11 = (bf16[1024,512]{1,0:T(8,128)(2,1)S(1)}, bf16[1024,512]{1,0:T(8,128)(2,1)}, u32[]{:S(2)}) copy-start(bf16[1024,512]{1,0:T(8,128)(2,1)} %param.9) | copy-start | bytes 3145732
  14.7 11.2 %copy-start.17 = (f32[2048]{0:T(1024)S(1)}, f32[2048]{0:T(1024)}, u32[]{:S(2)}) copy-start(f32[2048]{0:T(1024)} %param.11) | copy-start | bytes 24580
  20.5 5.5 %copy-start.21 = (f32[1024]{0:T(1024)}, f32[1024]{0:T(1024)S(1)}, u32[]{:S(2)}) copy-start(f32[1024]{0:T(1024)S(1)} %add_rsqrt_fusion.1) | copy-start | bytes 12292
  20.8 131.6 %collective-permute-start.1 = (bf16[1024,512]{0,1:T(8,128)(2,1)S(1)}, bf16[1024,512]{0,1:T(8,128)(2,1)}, u32[]{:S(2)}, u32[]{:S(2)}) collective-permute-start(bf16[1024,512]{0,1:T(8,128)(2,1)S(1)} %fusion.39), channel_id=1, source_target_pairs={{0,2},{2,4},{4,6},{6,8},{8,10},{10,12},{12,14},{14,16},{16,18},{18... | collective-permute-start | bytes 3145736 | tf_op jit(solution)/shard_map/ppermute | solution.py:20
  26.0 2.8 copy-start.19
  28.8 2.9 copy-start.13
  31.7 12.7 %copy-start.7 = (bf16[512,2048]{0,1:T(8,128)(2,1)}, bf16[512,2048]{0,1:T(8,128)(2,1)S(1)}, u32[]{:S(2)}) copy-start(bf16[512,2048]{0,1:T(8,128)(2,1)S(1)} %get-tuple-element.97) | copy-start | bytes 6291460
  122.4 13.3 %copy-start.5 = (f32[4,1024,128,1]{1,2,3,0:T(8,128)S(1)}, f32[4,1024,128,1]{1,2,3,0:T(8,128)}, u32[]{:S(2)}) copy-start(f32[4,1024,128,1]{1,2,3,0:T(8,128)} %fusion.70) | copy-start | bytes 6291460
  137.5 10.3 %copy-start.12 = (bf16[1024,512]{1,0:T(8,128)(2,1)S(1)}, bf16[1024,512]{1,0:T(8,128)(2,1)}, u32[]{:S(2)}) copy-start(bf16[1024,512]{1,0:T(8,128)(2,1)} %param.9) | copy-start | bytes 3145732
  147.9 6.6 %copy-start.6 = (bf16[512,2048]{0,1:T(8,128)(2,1)S(1)}, bf16[512,2048]{0,1:T(8,128)(2,1)}, u32[]{:S(2)}) copy-start(bf16[512,2048]{0,1:T(8,128)(2,1)} %get-tuple-element.96) | copy-start | bytes 6291460
  173.7 12.3 %copy-start.23 = (f32[4,4,512]{2,1,0:T(4,128)}, f32[4,4,512]{2,1,0:T(4,128)S(1)}, u32[]{:S(2)}) copy-start(f32[4,4,512]{2,1,0:T(4,128)S(1)} %get-tuple-element.108) | copy-start | bytes 98308
  186.0 8.4 %copy-start.15 = (bf16[1024,512]{0,1:T(8,128)(2,1)S(1)}, bf16[1024,512]{0,1:T(8,128)(2,1)}, u32[]{:S(2)}) copy-start(bf16[1024,512]{0,1:T(8,128)(2,1)} %copy.40) | copy-start | bytes 3145732
  218.0 12.0 %copy-start.14 = (bf16[1024,512]{0,1:T(8,128)(2,1)S(1)}, bf16[1024,512]{0,1:T(8,128)(2,1)}, u32[]{:S(2)}) copy-start(bf16[1024,512]{0,1:T(8,128)(2,1)} %pad_maximum_fusion.2) | copy-start | bytes 3145732
  230.0 8.4 %copy-start.3 = (f32[4,128,4,512]{3,1,2,0:T(8,128)S(1)}, f32[4,128,4,512]{3,1,2,0:T(8,128)}, u32[]{:S(2)}) copy-start(f32[4,128,4,512]{3,1,2,0:T(8,128)} %broadcast_multiply_fusion) | copy-start | bytes 12582916
  239.3 5.4 %copy-start.8 = (bf16[4,4,512,128]{2,3,1,0:T(8,128)(2,1)S(1)}, bf16[4,4,512,128]{2,3,1,0:T(8,128)(2,1)}, u32[]{:S(2)}) copy-start(bf16[4,4,512,128]{2,3,1,0:T(8,128)(2,1)} %get-tuple-element.111) | copy-start | bytes 6291460
  239.3 5.4 %copy-start.9 = (bf16[4,128,4,512]{3,1,2,0:T(8,128)(2,1)S(1)}, bf16[4,128,4,512]{3,1,2,0:T(8,128)(2,1)}, u32[]{:S(2)}) copy-start(bf16[4,128,4,512]{3,1,2,0:T(8,128)(2,1)} %get-tuple-element.113) | copy-start | bytes 6291460
  255.8 145.0 %collective-permute-start.3 = (f32[512,512]{1,0:T(8,128)}, f32[512,512]{1,0:T(8,128)}, u32[]{:S(2)}, u32[]{:S(2)}) collective-permute-start(f32[512,512]{1,0:T(8,128)} %copy.66), channel_id=1, source_target_pairs={{2,0},{4,2},{6,4},{8,6},{10,8},{12,10},{14,12},{16,14},{18,16},{20... | collective-permute-start | bytes 3145736 | tf_op jit(solution)/shard_map/ppermute | solution.py:20
  257.1 48.3 %collective-permute-start.2 = (f32[512,512]{0,1:T(8,128)}, f32[512,512]{0,1:T(8,128)}, u32[]{:S(2)}, u32[]{:S(2)}) collective-permute-start(f32[512,512]{0,1:T(8,128)} %bitcast.187), channel_id=1, source_target_pairs={{2,0},{4,2},{6,4},{8,6},{10,8},{12,10},{14,12},{16,14},{18,16},{20... | collective-permute-start | bytes 3145736 | tf_op jit(solution)/shard_map/ppermute | solution.py:20
  261.3 3.3 copy-start.4
  263.7 1.5 copy-start.10
  263.7 3.2 copy-start
  263.7 3.2 copy-start.18
  263.7 3.2 copy-start.20
  271.4 35.6 %copy-start.2 = (bf16[1024,512]{0,1:T(8,128)(2,1)S(1)}, bf16[1024,512]{0,1:T(8,128)(2,1)}, u32[]{:S(2)}) copy-start(bf16[1024,512]{0,1:T(8,128)(2,1)} %copy-done.1) | copy-start | bytes 3145732
  271.4 35.6 %copy-start.22 = (f32[1024]{0:T(1024)S(1)}, f32[1024]{0:T(1024)}, u32[]{:S(2)}) copy-start(f32[1024]{0:T(1024)} %copy-done.21) | copy-start | bytes 12292
  271.4 35.6 %copy-start.25 = (f32[512]{0:T(512)S(1)}, f32[512]{0:T(512)}, u32[]{:S(2)}) copy-start(f32[512]{0:T(512)} %param.12) | copy-start | bytes 6148
  325.1 77.4 %copy-start.16 = (bf16[512,512]{1,0:T(8,128)(2,1)S(1)}, bf16[512,512]{1,0:T(8,128)(2,1)}, u32[]{:S(2)}) copy-start(bf16[512,512]{1,0:T(8,128)(2,1)} %slice.83) | copy-start | bytes 1572868
where the time goes:
time: 407 us; the launch traced here: 404 us
  matrix products  161 us (40%)
  blocking collectives  78.3 us (19%)
  other arithmetic  61.3 us (15%)
  local copies, waits for them, and re-layouts  55.8 us (14%)
  waiting for transfers between devices  34 us (8%)
  starting transfers between devices  12.3 us (3%)
    psum x1, blocking collectives, local(): lax.psum((jnp.sum(dquery * query_unit, axis=0), jnp.sum(dkey * key_unit_r...  73.3 us
    dot_general x2, matrix products, attend(): jnp.einsum('ighd,jgd->ghij', gradient_block, value_block, preferred_eleme...  48.9 us
    sub x2, matrix products, attend(): expo = jnp.where(visible, jnp.exp(scores - row_max), 0.0)  38.8 us
    ppermute x4, waiting for transfers between devices, from_behind(): return lax.ppermute(array, axis, pairs)  34 us
    unnamed x60, local copies, waits for them, and re-layouts  28 us
    dot_general x2, matrix products, attend(): jnp.einsum('ghij,ighd->jgd', dscores_low, query_block, preferred_element_...  25.3 us
    convert_element_type x2, other arithmetic, attend(): weights_low = weights.astype(jnp.bfloat16)  24.6 us
    dot_general x2, matrix products, attend(): jnp.einsum('ghij,jgd->ighd', dscores_low, key_block, preferred_element_ty...  18.7 us
  transfers between devices with their start and end apart: 4, of which 1 were waited for; matrix products, arithmetic and copies ran while one was open for 42% of the time, Pallas kernels for 0%

commit v1 on v0

v1 whole, which is shorter than its diff:
```python
import functools

import jax
import jax.numpy as jnp
from jax import lax
from jax.experimental import pallas as pl
from jax.experimental.pallas import tpu as pltpu
from jax.sharding import PartitionSpec as P


QUERY_HEADS = 32
KEY_VALUE_HEADS = 8
HEAD_SIZE = 128
WINDOW_REACH = 512
BLOCK = 128

EPS = 1e-06
NEGATIVE = -1e30
LOG2_E = 1.4426950408889634
SOFTMAX_SCALE = HEAD_SIZE ** (-0.5)
SPAN = WINDOW_REACH + BLOCK
BACK = WINDOW_REACH // BLOCK
PAIR = 2 * HEAD_SIZE


def side_by_side(stacked, group):
    return jnp.concatenate([stacked[h * BLOCK : (h + 1) * BLOCK] for h in range(group)], axis=1)


def on_top(tile, group):
    return jnp.concatenate(
        [tile[:, h * HEAD_SIZE : (h + 1) * HEAD_SIZE] for h in range(group)], axis=0
    )


def as_columns(row):
    return jnp.transpose(jnp.broadcast_to(row, (BLOCK, BLOCK)))


def query_scale(summed):
    return lax.rsqrt(summed * (1.0 / (QUERY_HEADS * HEAD_SIZE)) + EPS)


def key_scale(summed):
    return lax.rsqrt(summed * (1.0 / (KEY_VALUE_HEADS * HEAD_SIZE)) + EPS)


def fold_rows(tile):
    folded = tile[:, :HEAD_SIZE]
    for h in range(1, tile.shape[1] // HEAD_SIZE):
        folded = folded + tile[:, h * HEAD_SIZE : (h + 1) * HEAD_SIZE]
    return jnp.sum(jnp.transpose(folded), axis=0, keepdims=True)


def attention_kernel(group, chunk, chunks, passed, begun, *refs):
    (
        docs_ref,
        q_ref,
        q_scale_ref,
        q_gain_ref,
        grad_ref,
        k_lo_ref,
        k_hi_ref,
        lo_scale_ref,
        hi_scale_ref,
        k_gain_ref,
        v_lo_ref,
        v_hi_ref,
    ) = refs[:12]
    refs = refs[12:]
    prior_gain_ref, prior_dots_ref = None, None
    if begun[0]:
        prior_gain_ref, refs = refs[0], refs[1:]
    if begun[1]:
        prior_dots_ref, refs = refs[0], refs[1:]
    refs = refs[passed:]
    (
        out_ref,
        dq_ref,
        hi_ref,
        gain_grad_ref,
        dots_ref,
        lo_ref,
        k_scr,
        v_scr,
        kt_scr,
        vt_scr,
        unit_scr,
        dk_scr,
        dv_scr,
    ) = refs
    f32, bf16 = jnp.float32, jnp.bfloat16
    q_gain = q_gain_ref[...]
    k_gain = k_gain_ref[...]

    for half, (raw_ref, scale_ref, val_ref) in enumerate(
        ((k_lo_ref, lo_scale_ref, v_lo_ref), (k_hi_ref, hi_scale_ref, v_hi_ref))
    ):
        for j in range(BACK):
            src = slice(j * BLOCK, (j + 1) * BLOCK)
            dst = slice((half * BACK + j) * BLOCK, (half * BACK + j + 1) * BLOCK)
            unit = raw_ref[src, :].astype(f32) * as_columns(key_scale(scale_ref[j]))
            unit_scr[dst, :] = unit
            norm = (unit * k_gain).astype(bf16)
            k_scr[dst, :] = norm
            kt_scr[:, dst] = jnp.transpose(norm)
            vals = val_ref[src, :]
            v_scr[dst, :] = vals
            vt_scr[:, dst] = jnp.transpose(vals)
    dk_scr[...] = jnp.zeros_like(dk_scr)
    dv_scr[...] = jnp.zeros_like(dv_scr)

    def mask():
        key_pos = lax.broadcasted_iota(jnp.int32, (BLOCK, BLOCK), 0)
        query_pos = lax.broadcasted_iota(jnp.int32, (BLOCK, BLOCK), 1)
        return jnp.concatenate([key_pos <= query_pos] * group, axis=1)

    def split_edge(parts):
        causal = mask()
        zero = jnp.zeros_like(parts[0])
        return jnp.concatenate(
            [jnp.where(causal, zero, parts[0])]
            + parts[1:]
            + [jnp.where(causal, parts[0], zero)],
            axis=0,
        ).astype(bf16)

    def forward(step):
        rows = slice(step * BLOCK, (step + 1) * BLOCK)
        window = slice(step * BLOCK, step * BLOCK + SPAN)
        scale = jnp.concatenate([as_columns(query_scale(q_scale_ref[step]))] * group, axis=1)
        unit = q_ref[rows, :].astype(f32) * scale
        queries = on_top((unit * q_gain).astype(bf16), group)
        place = chunk * BACK + step
        seen = [docs_ref[place + j] == docs_ref[place + BACK] for j in range(BACK)]
        scores = lax.dot_general(
            k_scr[window, :], queries, (((1,), (1,)), ((), ())), preferred_element_type=f32
        )
        part = [scores[j * BLOCK : (j + 1) * BLOCK] for j in range(BACK + 1)]
        edge = jnp.where(mask(), part[BACK], part[0] + jnp.where(seen[0], 0.0, NEGATIVE))
        top = jnp.max(edge, axis=0, keepdims=True)
        for j in range(1, BACK):
            top = jnp.maximum(
                top,
                jnp.max(part[j], axis=0, keepdims=True) + jnp.where(seen[j], 0.0, NEGATIVE),
            )
        factor = SOFTMAX_SCALE * LOG2_E
        expo = [jnp.exp2((edge - top) * factor)]
        for j in range(1, BACK):
            lift = top + jnp.where(seen[j], 0.0, -NEGATIVE)
            expo.append(jnp.exp2((part[j] - lift) * factor))
        total = jnp.sum(expo[0], axis=0, keepdims=True)
        for j in range(1, BACK):
            total = total + jnp.sum(expo[j], axis=0, keepdims=True)
        inverse = 1.0 / total
        weights = [e * inverse for e in expo]
        return queries, weights

    def backward(step, state):
        queries, weights = state
        rows = slice(step * BLOCK, (step + 1) * BLOCK)
        window = slice(step * BLOCK, step * BLOCK + SPAN)
        grads = on_top(grad_ref[rows, :], group)
        grads_t = jnp.transpose(grads)
        weights_low = split_edge(weights)
        out_t = jnp.dot(vt_scr[:, window], weights_low, preferred_element_type=f32).astype(bf16)
        delta = jnp.sum(grads_t.astype(f32) * out_t.astype(f32), axis=0, keepdims=True)
        out_ref[rows, :] = side_by_side(jnp.transpose(out_t), group)
        dweights = jnp.dot(v_scr[window, :], grads_t, preferred_element_type=f32)
        dpart = [dweights[j * BLOCK : (j + 1) * BLOCK] for j in range(BACK + 1)]
        dpart[0] = jnp.where(mask(), dpart[BACK], dpart[0])
        dscores_low = split_edge([weights[j] * (dpart[j] - delta) for j in range(BACK)])
        dv_scr[window, :] += jnp.dot(weights_low, grads, preferred_element_type=f32)
        dk_scr[window, :] += jnp.dot(dscores_low, queries, preferred_element_type=f32)
        dq_t = jnp.dot(kt_scr[:, window], dscores_low, preferred_element_type=f32)
        dquery = side_by_side(jnp.transpose(dq_t), group) * SOFTMAX_SCALE
        scale = jnp.concatenate([as_columns(query_scale(q_scale_ref[step]))] * group, axis=1)
        unit = q_ref[rows, :].astype(f32) * scale
        gained = dquery * q_gain
        dq_ref[rows, :] = gained.astype(bf16)
        query_dots.append(fold_rows(gained * unit))
        return jnp.sum(dquery * unit, axis=0, keepdims=True)

    steps = q_ref.shape[0] // BLOCK
    query_dots = []
    total = jnp.zeros((1, group * HEAD_SIZE), f32)
    if PIPELINE:
        state = forward(0)
        for step in range(steps):
            following = forward(step + 1) if step + 1 < steps else None
            total = total + backward(step, state)
            state = following
    else:
        for step in range(steps):
            total = total + backward(step, forward(step))
    width = group * HEAD_SIZE

    key_total = jnp.zeros((1, HEAD_SIZE), f32)
    key_dots = []
    for half, ref in enumerate((lo_ref, hi_ref)):
        for j in range(BACK):
            dst = slice(j * BLOCK, (j + 1) * BLOCK)
            src = slice((half * BACK + j) * BLOCK, (half * BACK + j + 1) * BLOCK)
            dkey = dk_scr[src, :] * SOFTMAX_SCALE
            gained = dkey * unit_scr[src, :]
            key_total = key_total + jnp.sum(gained, axis=0, keepdims=True)
            key_dots.append(fold_rows(gained * k_gain))
            ref[dst, :HEAD_SIZE] = dkey.astype(ref.dtype)
            ref[dst, HEAD_SIZE:] = dv_scr[src, :].astype(ref.dtype)
    if prior_gain_ref is not None:
        total = total + prior_gain_ref[:, :width]
        key_total = key_total + prior_gain_ref[:, width:]
    gain_grad_ref[:, :width] = total
    gain_grad_ref[:, width:] = key_total

    @pl.when(pl.program_id(0) == 0)
    def _():
        if prior_dots_ref is None:
            dots_ref[...] = jnp.zeros_like(dots_ref)
        else:
            dots_ref[...] = prior_dots_ref[...]

    for step in range(steps):
        dots_ref[chunk * BACK + step] += query_dots[step]
    for j in range(0 if chunk else BACK, 2 * BACK):
        dots_ref[(chunks + chunk - 1) * BACK + j] += key_dots[j]


PIPELINE = True


def attention(
    docs, q_raw, q_scale, q_gain, grad, lo, hi, k_gain, passed, chunk, heads, own_lo, begun
):
    tok_rows, query_cols = q_raw.shape
    key_cols = k_gain.shape[1]
    group = query_cols // key_cols
    width = group * HEAD_SIZE
    lowest, count = heads
    f32, bf16 = jnp.float32, jnp.bfloat16
    rows_spec = pl.BlockSpec((WINDOW_REACH, width), lambda g: (chunk, lowest + g))
    scale_spec = lambda block: pl.BlockSpec((BACK, 1, BLOCK), lambda g: (block, 0, 0))
    key_spec = lambda block, col: pl.BlockSpec((WINDOW_REACH, HEAD_SIZE), lambda g: (block, col + g))
    pair_spec = pl.BlockSpec((WINDOW_REACH, PAIR), lambda g: (0, lowest + g))
    own_pair_spec = pl.BlockSpec((WINDOW_REACH, PAIR), lambda g: (0, g))
    gain_spec = pl.BlockSpec((1, width + HEAD_SIZE), lambda g: (0, lowest + g))
    blocks = tok_rows // BLOCK
    whole_spec = pl.BlockSpec((2 * blocks, 1, BLOCK), lambda g: (0, 0, 0))
    operands = [docs, q_raw, q_scale, q_gain, grad, lo[0], hi[0], lo[1], hi[1], k_gain, lo[5], hi[5]]
    in_specs = [
        pl.BlockSpec(memory_space=pltpu.SMEM),
        rows_spec,
        scale_spec(chunk),
        pl.BlockSpec((1, width), lambda g: (0, lowest + g)),
        rows_spec,
        key_spec(lo[2], lo[3]),
        key_spec(hi[2], hi[3]),
        scale_spec(lo[2]),
        scale_spec(hi[2]),
        pl.BlockSpec((1, HEAD_SIZE), lambda g: (0, lowest + g)),
        key_spec(lo[2], lo[4]),
        key_spec(hi[2], hi[4]),
    ]
    outs = [
        (rows_spec, (tok_rows, query_cols), bf16),
        (rows_spec, (tok_rows, query_cols), bf16),
        (pair_spec, (WINDOW_REACH, 2 * key_cols), bf16),
        (gain_spec, (1, query_cols + key_cols), f32),
        (whole_spec, (2 * blocks, 1, BLOCK), f32),
        (own_pair_spec, (WINDOW_REACH, count * PAIR), bf16)
        if own_lo
        else (pair_spec, (WINDOW_REACH, 2 * key_cols), bf16),
    ]
    aliases, extra = {}, []
    for index, spec in ((3, gain_spec), (4, whole_spec)):
        if begun[index - 3]:
            aliases[len(operands)] = index
            operands.append(passed[index])
            in_specs.append(spec)
    for index, array in enumerate(passed):
        if array is not None and index not in aliases.values():
            aliases[len(operands) + len(extra)] = index
            extra.append(array)
    return pl.pallas_call(
        functools.partial(
            attention_kernel, group, chunk, blocks // BACK, len(extra), begun
        ),
        grid=(count,),
        in_specs=in_specs + [pl.BlockSpec(memory_space=pl.ANY)] * len(extra),
        out_specs=[o[0] for o in outs],
        out_shape=[jax.ShapeDtypeStruct(o[1], o[2]) for o in outs],
        input_output_aliases=aliases,
        scratch_shapes=[
            pltpu.VMEM((2 * WINDOW_REACH, HEAD_SIZE), bf16),
            pltpu.VMEM((2 * WINDOW_REACH, HEAD_SIZE), bf16),
            pltpu.VMEM((HEAD_SIZE, 2 * WINDOW_REACH), bf16),
            pltpu.VMEM((HEAD_SIZE, 2 * WINDOW_REACH), bf16),
            pltpu.VMEM((2 * WINDOW_REACH, HEAD_SIZE), f32),
            pltpu.VMEM((2 * WINDOW_REACH, HEAD_SIZE), f32),
            pltpu.VMEM((2 * WINDOW_REACH, HEAD_SIZE), f32),
        ],
        cost_estimate=pl.CostEstimate(
            flops=12 * WINDOW_REACH * count * width * SPAN,
            bytes_accessed=WINDOW_REACH * count * (8 * width + 16 * HEAD_SIZE),
            transcendentals=WINDOW_REACH * count * group * WINDOW_REACH,
        ),
        name="halo_attention" if own_lo else "attention",
    )(*operands, *extra)


def back_dot_kernel(raw_ref, scale_ref, gain_ref, dots_ref, *refs):
    backs, out_ref = refs[:-1], refs[-1]
    out_ref[...] = dots_ref[...]
    first = dots_ref.shape[0] - BACK
    for j in range(BACK):
        rows = slice(j * BLOCK, (j + 1) * BLOCK)
        index = first + j
        total = jnp.zeros((BLOCK, BLOCK), jnp.float32)
        head = 0
        for back in backs:
            for h in range(back.shape[1] // PAIR):
                cols = slice(head * HEAD_SIZE, (head + 1) * HEAD_SIZE)
                grad = back[rows, h * PAIR : h * PAIR + HEAD_SIZE].astype(jnp.float32)
                total = total + grad * gain_ref[:, cols] * raw_ref[rows, cols].astype(jnp.float32)
                head += 1
        out_ref[index] = dots_ref[index] + fold_rows(total * as_columns(key_scale(scale_ref[j])))


def add_back_dots(key_raw, k_scale, k_gain, dots, backs):
    tok_rows, key_cols = key_raw.shape
    last = tok_rows // WINDOW_REACH - 1
    return pl.pallas_call(
        back_dot_kernel,
        grid=(1,),
        in_specs=[
            pl.BlockSpec((WINDOW_REACH, key_cols), lambda g: (last, 0)),
            pl.BlockSpec((BACK, 1, BLOCK), lambda g: (last, 0, 0)),
            pl.BlockSpec((1, key_cols), lambda g: (0, 0)),
            pl.BlockSpec(dots.shape, lambda g: (0, 0, 0)),
        ]
        + [pl.BlockSpec(back.shape, lambda g: (0, 0)) for back in backs],
        out_specs=pl.BlockSpec(dots.shape, lambda g: (0, 0, 0)),
        out_shape=jax.ShapeDtypeStruct(dots.shape, jnp.float32),
        name="back_dots",
    )(key_raw, k_scale, k_gain, dots, *backs)


def finish_kernel(group, chunks, passed, *refs):
    f32 = jnp.float32
    (u_ref, q_ref, q_scale_ref, k_ref, k_scale_ref, k_gain_ref, dots_ref), refs = refs[:7], refs[7:]
    highs, refs = refs[:chunks], refs[chunks:]
    lows, refs = refs[: chunks - 1], refs[chunks - 1 :]
    back, refs = refs[0], refs[1 + passed :]
    q_out, k_out, v_out, qa_scr, qd_scr, ka_scr, kd_scr = refs
    g = pl.program_id(0)
    blocks = chunks * BACK

    @pl.when(g == 0)
    def _():
        for b in range(blocks):
            rows = slice(b * BLOCK, (b + 1) * BLOCK)
            dot = dots_ref[b]
            qa_scr[rows, :] = as_columns(query_scale(q_scale_ref[b]))
            qd_scr[rows, :] = as_columns(dot * (1.0 / (QUERY_HEADS * HEAD_SIZE)))
            dot = dots_ref[blocks + b]
            ka_scr[rows, :] = as_columns(key_scale(k_scale_ref[b]))
            kd_scr[rows, :] = as_columns(dot * (1.0 / (KEY_VALUE_HEADS * HEAD_SIZE)))

    for b in range(blocks):
        rows = slice(b * BLOCK, (b + 1) * BLOCK)
        scale, dot = qa_scr[rows, :], qd_scr[rows, :]
        for h in range(group):
            cols = slice(h * HEAD_SIZE, (h + 1) * HEAD_SIZE)
            unit = q_ref[rows, cols].astype(f32) * scale
            q_out[rows, cols] = (scale * (u_ref[rows, cols].astype(f32) - unit * dot)).astype(
                q_out.dtype
            )
    for b in range(blocks):
        rows = slice(b * BLOCK, (b + 1) * BLOCK)
        chunk, j = divmod(b, BACK)
        src = slice(j * BLOCK, (j + 1) * BLOCK)
        grad = highs[chunk][src, :].astype(f32)
        if chunk < chunks - 1:
            grad = grad + lows[chunk][src, :].astype(f32)
        else:
            grad = grad + back[src, :].astype(f32)
        scale, dot = ka_scr[rows, :], kd_scr[rows, :]
        unit = k_ref[rows, :].astype(f32) * scale
        k_out[rows, :] = (
            scale * (grad[:, :HEAD_SIZE] * k_gain_ref[...] - unit * dot)
        ).astype(k_out.dtype)
        v_out[rows, :] = grad[:, HEAD_SIZE:].astype(v_out.dtype)


def finish(scaled, q_raw, q_scale, key_raw, k_scale, k_gain, dots, highs, lows, back, heads, passed):
    tok_rows, query_cols = q_raw.shape
    key_cols = key_raw.shape[1]
    group = query_cols // key_cols
    chunks = tok_rows // WINDOW_REACH
    lowest, count = heads
    queries = pl.BlockSpec((tok_rows, group * HEAD_SIZE), lambda g: (0, lowest + g))
    keys = pl.BlockSpec((tok_rows, HEAD_SIZE), lambda g: (0, lowest + g))
    pairs = pl.BlockSpec((WINDOW_REACH, PAIR), lambda g: (0, lowest + g))
    fixed = lambda array: pl.BlockSpec(array.shape, lambda g: (0, 0, 0))
    bf16 = jnp.bfloat16
    operands = [scaled, q_raw, q_scale, key_raw, k_scale, k_gain, dots, *highs, *lows, back]
    return pl.pallas_call(
        functools.partial(finish_kernel, group, chunks, len(passed)),
        grid=(count,),
        in_specs=[
            queries,
            queries,
            fixed(q_scale),
            keys,
            fixed(k_scale),
            pl.BlockSpec((1, HEAD_SIZE), lambda g: (0, lowest + g)),
            fixed(dots),
        ]
        + [pairs] * (len(highs) + len(lows))
        + [pl.BlockSpec((WINDOW_REACH, PAIR), lambda g: (0, g))]
        + [pl.BlockSpec(memory_space=pl.ANY)] * len(passed),
        out_specs=[queries, keys, keys],
        out_shape=[
            jax.ShapeDtypeStruct((tok_rows, query_cols), bf16),
            jax.ShapeDtypeStruct((tok_rows, key_cols), bf16),
            jax.ShapeDtypeStruct((tok_rows, key_cols), bf16),
        ],
        input_output_aliases={len(operands) + i: i for i in range(len(passed))},
        scratch_shapes=[pltpu.VMEM((tok_rows, HEAD_SIZE), jnp.float32)] * 4,
        cost_estimate=pl.CostEstimate(
            flops=8 * tok_rows * count * group * HEAD_SIZE,
            bytes_accessed=tok_rows * count * HEAD_SIZE * (6 * group + 12),
            transcendentals=0,
        ),
        name="finish",
    )(*operands, *passed)


def square_kernel(q_ref, k_ref, q_out, k_out):
    for ref, out in ((q_ref, q_out), (k_ref, k_out)):
        for j in range(ref.shape[0] // BLOCK):
            tile = ref[j * BLOCK : (j + 1) * BLOCK, :].astype(jnp.float32)
            out[j] = fold_rows(tile * tile)


def row_squares(q_raw, key_raw):
    tok_rows = q_raw.shape[0]
    step = 2 * BLOCK
    blocks = tok_rows // BLOCK
    shape = jax.ShapeDtypeStruct((blocks, 1, BLOCK), jnp.float32)
    out = pl.BlockSpec((step // BLOCK, 1, BLOCK), lambda i: (i, 0, 0))
    return pl.pallas_call(
        square_kernel,
        grid=(tok_rows // step,),
        in_specs=[pl.BlockSpec((step, a.shape[1]), lambda i: (i, 0)) for a in (q_raw, key_raw)],
        out_specs=[out, out],
        out_shape=[shape, shape],
        name="row_squares",
    )(q_raw, key_raw)


def from_behind(array, axis, by):
    peers = lax.axis_size(axis)
    pairs = [(i, i + by) for i in range(peers) if 0 <= i + by < peers]
    return lax.ppermute(array, axis, pairs)


def sum_over(array, axis):
    peers = lax.axis_size(axis)
    if peers & (peers - 1):
        return lax.psum(array, axis)
    rounds = peers.bit_length() - 1
    for index in range(rounds):
        moved = lax.ppermute(array, axis, [(i, i ^ (1 << index)) for i in range(peers)])
        array = array + moved
    return array


def whole(query_raw, key_raw, values, output_gradient, query_gain, key_norm_gain, block_docs):
    tok_rows, query_cols = query_raw.shape
    key_cols = key_raw.shape[1]
    kv_heads = key_cols // HEAD_SIZE
    width = query_cols // kv_heads
    tail = tok_rows - WINDOW_REACH
    half = max(1, kv_heads // 2)
    shares = [(0, half)] + ([(half, kv_heads - half)] if kv_heads > half else [])
    halo = from_behind(jnp.concatenate([key_raw[tail:], values[tail:]], axis=1), "ctx", 1)
    q_scale, k_scale = lax.psum(row_squares(query_raw, key_raw), "head")
    halo_scale = from_behind(k_scale[tail // BLOCK :], "ctx", 1)
    q_gain = query_gain.reshape(1, query_cols)
    k_gain = key_norm_gain.reshape(1, key_cols)
    docs = lax.dynamic_slice_in_dim(
        jnp.concatenate([jnp.full((BACK,), -1, jnp.int32), block_docs]),
        lax.axis_index("ctx") * (tok_rows // BLOCK),
        BACK + tok_rows // BLOCK,
        0,
    )

    chunks = tok_rows // WINDOW_REACH
    state = {"rows": [None, None], "gains": None, "dots": None}
    highs, lows, backs, touched = [None] * chunks, [None] * chunks, [], set()

    def run(chunk, share):
        lowest, count = shares[share]
        if chunk == 0:
            lo = (halo, halo_scale, 0, lowest, kv_heads + lowest, halo)
        else:
            lo = (key_raw, k_scale, chunk - 1, lowest, lowest, values)
        passed = state["rows"] + [highs[chunk], state["gains"], state["dots"]]
        if chunk > 0:
            passed.append(lows[chunk])
        result = attention(
            docs, query_raw, q_scale, q_gain, output_gradient,
            lo, (key_raw, k_scale, chunk, lowest, lowest, values),
            k_gain, passed, chunk, (lowest, count), chunk == 0,
            (share in touched, state["dots"] is not None),
        )
        touched.add(share)
        state["rows"] = list(result[:2])
        highs[chunk], state["gains"], state["dots"] = result[2:5]
        if chunk == 0:
            backs.append(from_behind(result[5], "ctx", -1))
        else:
            lows[chunk] = result[5]

    for chunk in range(1, chunks):
        run(chunk, 0)
    for share in range(len(shares)):
        run(0, share)
    for chunk in range(1, chunks):
        for share in range(1, len(shares)):
            run(chunk, share)
    attended, query_scaled = state["rows"]
    dots = add_back_dots(key_raw, k_scale, k_gain, state["dots"], backs)
    dots = lax.psum(dots, "head")
    finished = []
    for share, heads in enumerate(shares):
        finished = list(
            finish(
                query_scaled, query_raw, q_scale, key_raw, k_scale, k_gain,
                dots, highs, lows[1:], backs[share], heads, finished,
            )
        )
    query_grad, key_raw_gradient, value_grad = finished
    gain_grads = sum_over(state["gains"], "ctx").reshape(kv_heads, -1)
    return (
        attended,
        query_grad,
        key_raw_gradient,
        value_grad,
        gain_grads[:, :width].reshape(query_cols),
        gain_grads[:, width:].reshape(key_cols),
    )


def solution(mesh):
    placed = (
        P("ctx", "head"),
        P("ctx", "head"),
        P("ctx", "head"),
        P("ctx", "head"),
        P("head"),
        P("head"),
        P(),
    )
    return jax.shard_map(
        whole,
        mesh=mesh,
        in_specs=placed,
        out_specs=(
            P("ctx", "head"),
            P("ctx", "head"),
            P("ctx", "head"),
            P("ctx", "head"),
            P("head"),
            P("head"),
        ),
        check_vma=False,
    )
```

time: 407 us -> 127 us (0.31)
  matrix products: 161 us -> 0 us
  blocking collectives: 78.3 us -> 6.35 us
  Pallas kernels: 0 us -> 68.1 us
  other arithmetic: 61.3 us -> 0.88 us
  local copies, waits for them, and re-layouts: 55.8 us -> 5.78 us
  waiting for transfers between devices: 34 us -> 24.4 us
  starting transfers between devices: 12.3 us -> 19.9 us
    dot_general x10 -> x0, matrix products: 122 us -> none  [the longest x2 48.9 us: attend(): jnp.einsum('ighd,jgd->ghij', gradient_block, value_block, preferred_eleme...]
    psum x3 -> x2, blocking collectives: 78.3 us -> 6.35 us  [the longest x1 3.18 us: whole(): q_scale, k_scale = lax.psum(row_squares(query_raw, key_raw), 'head')]
    pallas_call x0 -> x8, Pallas kernels: none -> 68.1 us  [the longest x4 50.6 us: attention(): pl.pallas_call(functools.partial(attention_kernel, group, chunk, blocks /...]
    sub x2 -> x0, matrix products: 38.8 us -> none  [attend(): expo = jnp.where(visible, jnp.exp(scores - row_max), 0.0)]
    convert_element_type x6 -> x0, other arithmetic: 36.2 us -> none  [the longest x2 24.6 us: attend(): weights_low = weights.astype(jnp.bfloat16)]
    unnamed x60 -> x18, local copies, waits for them, and re-layouts: 28 us -> 2.44 us
    ppermute x4, waiting for transfers between devices: 34 us -> 18.3 us  [from_behind(): return lax.ppermute(array, axis, pairs)]
    reshape x4 -> x2, local copies, waits for them, and re-layouts: 10.1 us -> 0.59 us  [the longest x1 0.58 us: whole(): gain_grads[:, width:].reshape(key_cols)]
  transfers between devices with their start and end apart: 4 -> 8, of which waited for: 1 -> 5; matrix products, arithmetic and copies ran while one was open for 42% -> 1% of each run, Pallas kernels for 0% -> 13%
where the time goes in v1:
time: 127 us; the launch traced here: 126 us
  Pallas kernels  68.1 us (54%)
  waiting for transfers between devices  24.4 us (19%)
  starting transfers between devices  19.9 us (16%)
  blocking collectives  6.35 us (5%)
  local copies, waits for them, and re-layouts  5.78 us (5%)
    pallas_call x4, Pallas kernels, attention(): pl.pallas_call(functools.partial(attention_kernel, group, chunk, blocks /...  50.6 us
    ppermute x4, waiting for transfers between devices, from_behind(): return lax.ppermute(array, axis, pairs)  18.3 us
    ppermute x4, starting transfers between devices, from_behind(): return lax.ppermute(array, axis, pairs)  10.8 us
    pallas_call x2, Pallas kernels, finish(): pl.pallas_call(functools.partial(finish_kernel, group, chunks, len(passed...  10.8 us
    ppermute x4, starting transfers between devices, sum_over(): lax.ppermute(array, axis, [(i, i ^ 1 << index) for i in range(peers)])  9.02 us
    ppermute x4, waiting for transfers between devices, sum_over(): lax.ppermute(array, axis, [(i, i ^ 1 << index) for i in range(peers)])  6.08 us
    pallas_call x1, Pallas kernels, row_squares(): pl.pallas_call(square_kernel, grid=(tok_rows // step,), in_specs=[pl.Bloc...  4.41 us
    psum x1, blocking collectives, whole(): q_scale, k_scale = lax.psum(row_squares(query_raw, key_raw), 'head')  3.18 us
  transfers between devices with their start and end apart: 8, of which 5 were waited for; matrix products, arithmetic and copies ran while one was open for 1% of the time, Pallas kernels for 13%

profile of v1, /device:TPU:0, one launch (start us, length us, event | category | flops | bytes accessed | tf_op | source)
XLA Modules:
  0.0 126.3 jit_solution(16913195317175648663)
XLA Ops:
  0.6 1.1 slice.16
  1.7 0.0 copy-start.7
  1.7 1.1 slice.15
  2.8 0.1 pad_maximum_fusion
  2.9 4.9 %collective-permute-start = (bf16[512,1024]{1,0:T(8,128)(2,1)S(1)}, bf16[512,1024]{1,0:T(8,128)(2,1)S(1)}, u32[]{:S(2)}, u32[]{:S(2)}) collective-permute-start(bf16[512,1024]{1,0:T(8,128)(2,1)S(1)} %pad_maximum_fusion), channel_id=1, source_target_pairs={{0,2},{2,4},{4,6},{6,8},{8,10},{10,12},{12,14},{14,16},{16,18},{18... | collective-permute-start | bytes 3145736 | tf_op jit(solution)/shard_map/ppermute | solution.py:465
  7.9 4.4 %row_squares.1 = (f32[8,1,128]{2,1,0:T(1,128)}, f32[8,1,128]{2,1,0:T(1,128)}) custom-call(bf16[1024,2048]{1,0:T(8,128)(2,1)} %refs_1_.11, bf16[1024,512]{1,0:T(8,128)(2,1)} %refs_3_.3), custom_call_target="tpu_custom_call" | custom-call | tf_op jit(solution)/shard_map/row_squares/pallas_call | solution.py:452
  12.3 3.2 %all-reduce.1 = (f32[8,1,128]{2,1,0:T(1,128)}, f32[8,1,128]{2,1,0:T(1,128)S(1)}) all-reduce(f32[8,1,128]{2,1,0:T(1,128)} %get-tuple-element.38, f32[8,1,128]{2,1,0:T(1,128)} %get-tuple-element.39), channel_id=1, replica_groups=mesh['ctx'=16,'head'=2] {'head'}, use_global_device_ids=true, to_apply=%region_0.0 | all-reduce | flops 2048 | bytes 16384 | tf_op jit(solution)/shard_map/psum | solution.py:488
  15.5 0.0 copy-start.3
  15.5 3.3 %collective-permute-start.1 = (f32[4,1,128]{2,1,0:T(1,128)S(1)}, f32[4,1,128]{2,1,0:T(1,128)S(1)}, u32[]{:S(2)}, u32[]{:S(2)}) collective-permute-start(f32[4,1,128]{2,1,0:T(1,128)S(1)} %slice.20), channel_id=1, source_target_pairs={{0,2},{2,4},{4,6},{6,8},{8,10},{10,12},{12,14},{14,16},{16,18},{18... | collective-permute-start | bytes 6152 | tf_op jit(solution)/shard_map/ppermute | solution.py:465
  18.8 0.0 copy-done.7
  18.8 0.6 pad_dynamic-slice_fusion.refs_0_
  19.4 0.0 copy-done.3
  19.4 12.6 %attention.2 = (bf16[1024,2048]{1,0:T(8,128)(2,1)}, bf16[1024,2048]{1,0:T(8,128)(2,1)}, bf16[512,1024]{1,0:T(8,128)(2,1)}, f32[1,2560]{1,0:T(1,128)}, f32[16,1,128]{2,1,0:T(1,128)}, /*index=5*/bf16[512,1024]{1,0:T(8,128)(2,1)}) custom-call(s32[12]{0:T(128)} %pad_dynamic-slice_fusion.refs_0_, bf16[1024,2048]{1,0:T(8,128)(2,1)} %refs_1_.11, ...), custom_call_target="tpu_custom_call" | custom-call | flops 4026531840 | bytes 6291456 | tf_op jit(solution)/shard_map/attention/pallas_call | solution.py:284
  32.0 0.0 collective-permute-done.1.refs_7_
  32.0 0.0 copy-start.4
  32.0 0.0 collective-permute-done.refs_5_.refs_10_
  32.0 0.0 copy-start
  32.0 0.5 copy-done.4
  32.6 0.4 copy-done
  33.0 12.6 %halo_attention.2 = (bf16[1024,2048]{1,0:T(8,128)(2,1)}, bf16[1024,2048]{1,0:T(8,128)(2,1)}, bf16[512,1024]{1,0:T(8,128)(2,1)}, f32[1,2560]{1,0:T(1,128)}, f32[1...) custom-call(s32[12]{0:T(128)} %pad_dynamic-slice_fusion.refs_0_, ...), custom_call_target="tpu_custom_call", output_to_operand_aliasing={{3}: (12, {}), {4}: (13, {}), {0}: (14, {}), {1}: (15, {})} | custom-call | flops 4026531840 | bytes 6291456 | tf_op jit(solution)/shard_map/halo_attention/pallas_call | solution.py:284
  45.6 12.8 %halo_attention.3 = (bf16[1024,2048]{1,0:T(8,128)(2,1)}, bf16[1024,2048]{1,0:T(8,128)(2,1)}, bf16[512,1024]{1,0:T(8,128)(2,1)}, f32[1,2560]{1,0:T(1,128)}, f32[1...) custom-call(s32[12]{0:T(128)} %pad_dynamic-slice_fusion.refs_0_, ...), custom_call_target="tpu_custom_call", output_to_operand_aliasing={{4}: (12, {}), {0}: (13, {}), {1}: (14, {}), {2}: (15, {}),... | custom-call | flops 4026531840 | bytes 6291456 | tf_op jit(solution)/shard_map/halo_attention/pallas_call | solution.py:284
  58.4 0.0 copy-start.6
  58.4 0.0 copy-start.5
  58.4 12.7 %attention.3 = (bf16[1024,2048]{1,0:T(8,128)(2,1)}, bf16[1024,2048]{1,0:T(8,128)(2,1)}, bf16[512,1024]{1,0:T(8,128)(2,1)}, f32[1,2560]{1,0:T(1,128)}, f32[16,1,128]{2,1,0:T(1,128)}, /*index=5*/bf16[512,1024]{1,0:T(8,128)(2,1)}) custom-call(s32[12]{0:T(128)} %pad_dynamic-slice_fusion.refs_0_, ...), custom_call_target="tpu_custom_call", output_to_operand_aliasing={{3}: (12, {}), {4}: (13, {}), {0}: (14, {}), {1}: (15, {}),... | custom-call | flops 4026531840 | bytes 6291456 | tf_op jit(solution)/shard_map/attention/pallas_call | solution.py:284
  71.1 1.6 %collective-permute-start.4 = (f32[1,2560]{1,0:T(1,128)}, f32[1,2560]{1,0:T(1,128)S(1)}, u32[]{:S(2)}, u32[]{:S(2)}) collective-permute-start(f32[1,2560]{1,0:T(1,128)} %get-tuple-element.69), channel_id=1, source_target_pairs={{0,2},{2,0},{4,6},{6,4},{8,10},{10,8},{12,14},{14,12},{16,18},{18,... | collective-permute-start | bytes 30728 | tf_op jit(solution)/shard_map/ppermute | solution.py:474
  72.6 2.4 %collective-permute-done.4 = f32[1,2560]{1,0:T(1,128)S(1)} collective-permute-done((f32[1,2560]{1,0:T(1,128)}, f32[1,2560]{1,0:T(1,128)S(1)}, u32[]{:S(2)}, u32[]{:S(2)}) %collective-permute-start.4) | collective-permute-done | bytes 10272 | tf_op jit(solution)/shard_map/ppermute | solution.py:474
  75.0 0.7 add.24
  75.7 1.7 %collective-permute-start.5 = (f32[1,2560]{1,0:T(1,128)S(1)}, f32[1,2560]{1,0:T(1,128)S(1)}, u32[]{:S(2)}, u32[]{:S(2)}) collective-permute-start(f32[1,2560]{1,0:T(1,128)S(1)} %add.24), channel_id=1, source_target_pairs={{0,4},{2,6},{4,0},{6,2},{8,12},{10,14},{12,8},{14,10},{16,20},{18,... | collective-permute-start | bytes 30728 | tf_op jit(solution)/shard_map/ppermute | solution.py:474
  77.4 2.0 %collective-permute-done.5 = f32[1,2560]{1,0:T(1,128)S(1)} collective-permute-done((f32[1,2560]{1,0:T(1,128)S(1)}, f32[1,2560]{1,0:T(1,128)S(1)}, u32[]{:S(2)}, u32[]{:S(2)}) %collective-permute-start.5) | collective-permute-done | bytes 10272 | tf_op jit(solution)/shard_map/ppermute | solution.py:474
  79.5 2.7 %collective-permute-start.6 = (f32[1,2560]{1,0:T(1,128)S(1)}, f32[1,2560]{1,0:T(1,128)S(1)}, u32[]{:S(2)}, u32[]{:S(2)}) collective-permute-start(f32[1,2560]{1,0:T(1,128)S(1)} %add.25), channel_id=1, source_target_pairs={{0,8},{2,10},{4,12},{6,14},{8,0},{10,2},{12,4},{14,6},{16,24},{18,... | collective-permute-start | bytes 30728 | tf_op jit(solution)/shard_map/ppermute | solution.py:474
  82.2 1.7 %collective-permute-done.6 = f32[1,2560]{1,0:T(1,128)S(1)} collective-permute-done((f32[1,2560]{1,0:T(1,128)S(1)}, f32[1,2560]{1,0:T(1,128)S(1)}, u32[]{:S(2)}, u32[]{:S(2)}) %collective-permute-start.6) | collective-permute-done | bytes 10272 | tf_op jit(solution)/shard_map/ppermute | solution.py:474
  83.8 3.1 %collective-permute-start.7 = (f32[1,2560]{1,0:T(1,128)S(1)}, f32[1,2560]{1,0:T(1,128)S(1)}, u32[]{:S(2)}, u32[]{:S(2)}) collective-permute-start(f32[1,2560]{1,0:T(1,128)S(1)} %add.26), channel_id=1, source_target_pairs={{0,16},{2,18},{4,20},{6,22},{8,24},{10,26},{12,28},{14,30},{16,0},... | collective-permute-start | bytes 30728 | tf_op jit(solution)/shard_map/ppermute | solution.py:474
  86.9 0.0 copy-done.6
  86.9 1.3 %collective-permute-start.3 = (bf16[512,512]{1,0:T(8,128)(2,1)S(1)}, bf16[512,512]{1,0:T(8,128)(2,1)S(1)}, u32[]{:S(2)}, u32[]{:S(2)}) collective-permute-start(bf16[512,512]{1,0:T(8,128)(2,1)S(1)} %copy-done.6), channel_id=1, source_target_pairs={{2,0},{4,2},{6,4},{8,6},{10,8},{12,10},{14,12},{16,14},{18,16},{20... | collective-permute-start | bytes 1572872 | tf_op jit(solution)/shard_map/ppermute | solution.py:465
  88.2 0.0 copy-done.5
  88.2 1.3 %collective-permute-start.2 = (bf16[512,512]{1,0:T(8,128)(2,1)S(1)}, bf16[512,512]{1,0:T(8,128)(2,1)S(1)}, u32[]{:S(2)}, u32[]{:S(2)}) collective-permute-start(bf16[512,512]{1,0:T(8,128)(2,1)S(1)} %copy-done.5), channel_id=1, source_target_pairs={{2,0},{4,2},{6,4},{8,6},{10,8},{12,10},{14,12},{16,14},{18,16},{20... | collective-permute-start | bytes 1572872 | tf_op jit(solution)/shard_map/ppermute | solution.py:465
  89.5 0.0 collective-permute-done.7
  89.6 0.6 copy.31
  90.2 0.6 slice_bitcast_fusion.1
  90.8 12.7 %collective-permute-done.3.refs_1_.refs_10_ = bf16[512,512]{1,0:T(8,128)(2,1)S(1)} collective-permute-done((bf16[512,512]{1,0:T(8,128)(2,1)S(1)}, bf16[512,512]{1,0:T(8,128)(2,1)S(1)}, u32[]{:S(2)}, u32[]{:S(2)}) %collective-permute-start.3) | collective-permute-done | bytes 524320 | tf_op jit(solution)/shard_map/ppermute | solution.py:465
  103.5 0.0 copy-start.1
  103.5 5.6 %collective-permute-done.2.refs_0_.refs_10_ = bf16[512,512]{1,0:T(8,128)(2,1)S(1)} collective-permute-done((bf16[512,512]{1,0:T(8,128)(2,1)S(1)}, bf16[512,512]{1,0:T(8,128)(2,1)S(1)}, u32[]{:S(2)}, u32[]{:S(2)}) %collective-permute-start.2) | collective-permute-done | bytes 524320 | tf_op jit(solution)/shard_map/ppermute | solution.py:465
  109.1 0.0 copy-done.1
  109.1 0.8 copy-done.2
  109.9 2.2 %back_dots.1 = f32[16,1,128]{2,1,0:T(1,128)} custom-call(bf16[1024,512]{1,0:T(8,128)(2,1)} %refs_3_.3, f32[8,1,128]{2,1,0:T(1,128)} %copy-done.3, f32[1,512]{1,0:T(1,128)} %bitcast.15, f32[16,1,128]{2,1,0:T(1,128)} %get-tuple-element.57.dots_ref, bf16[512,512]{1,0:T(8,128)(2,1)} %copy-done.2, bf16[512,512]{1,0:T(8,128)(2,1)} %copy-done.1), custom_call_target="tpu_custom_call" | custom-call | tf_op jit(solution)/shard_map/back_dots/pallas_call | solution.py:332
  112.2 3.2 %psum.23.refs_6_ = f32[16,1,128]{2,1,0:T(1,128)} all-reduce(f32[16,1,128]{2,1,0:T(1,128)} %back_dots.1), channel_id=1, replica_groups=mesh['ctx'=16,'head'=2] {'head'}, use_global_device_ids=true, to_apply=%region_2.0 | all-reduce | flops 2048 | bytes 16384 | tf_op jit(solution)/shard_map/psum | solution.py:535
  115.4 5.4 %finish.2 = (bf16[1024,2048]{1,0:T(8,128)(2,1)}, bf16[1024,512]{1,0:T(8,128)(2,1)}, bf16[1024,512]{1,0:T(8,128)(2,1)}) custom-call(bf16[1024,2048]{1,0:T(8,128)(2,1)} %get-tuple-element.56.refs_0_, bf16[1024,2048]{1,0:T(8,128)(2,1)} %refs_1_.11, f32[8,1,128]{2,1,0:T(1,128)} %get-tuple-element.70.refs_2_, bf16[1024,512]{1,0:T(8,128)(2,1)} %refs_3_.3, ...), custom_call_target="tpu_custom_call" | custom-call | flops 8388608 | bytes 9437184 | tf_op jit(solution)/shard_map/finish/pallas_call | solution.py:407
  120.8 5.4 %finish.3 = (bf16[1024,2048]{1,0:T(8,128)(2,1)}, bf16[1024,512]{1,0:T(8,128)(2,1)}, bf16[1024,512]{1,0:T(8,128)(2,1)}) custom-call(bf16[1024,2048]{1,0:T(8,128)(2,1)} %get-tuple-element.56.refs_0_, bf16[1024,2048]{1,0:T(8,128)(2,1)} %refs_1_.11, ...), custom_call_target="tpu_custom_call", output_to_operand_aliasing={{0}: (11, {}), {1}: (12, {}), {2}: (13, {})} | custom-call | flops 8388608 | bytes 9437184 | tf_op jit(solution)/shard_map/finish/pallas_call | solution.py:407
  (7 shorter events, 0.1 us)
Async XLA Ops:
  1.7 17.1 %copy-start.7 = (s32[128]{0:T(128)S(1)}, s32[128]{0:T(128)}, u32[]{:S(2)}) copy-start(s32[128]{0:T(128)} %param.13) | copy-start | bytes 1540
  2.9 29.1 %collective-permute-start = (bf16[512,1024]{1,0:T(8,128)(2,1)S(1)}, bf16[512,1024]{1,0:T(8,128)(2,1)S(1)}, u32[]{:S(2)}, u32[]{:S(2)}) collective-permute-start(bf16[512,1024]{1,0:T(8,128)(2,1)S(1)} %pad_maximum_fusion), channel_id=1, source_target_pairs={{0,2},{2,4},{4,6},{6,8},{8,10},{10,12},{12,14},{14,16},{16,18},{18... | collective-permute-start | bytes 3145736 | tf_op jit(solution)/shard_map/ppermute | solution.py:465
  15.5 3.9 %copy-start.3 = (f32[8,1,128]{2,1,0:T(1,128)}, f32[8,1,128]{2,1,0:T(1,128)S(1)}, u32[]{:S(2)}) copy-start(f32[8,1,128]{2,1,0:T(1,128)S(1)} %get-tuple-element.71.refs_7_.refs_8_.scale_ref.refs_4_) | copy-start | bytes 12292
  15.5 16.5 %collective-permute-start.1 = (f32[4,1,128]{2,1,0:T(1,128)S(1)}, f32[4,1,128]{2,1,0:T(1,128)S(1)}, u32[]{:S(2)}, u32[]{:S(2)}) collective-permute-start(f32[4,1,128]{2,1,0:T(1,128)S(1)} %slice.20), channel_id=1, source_target_pairs={{0,2},{2,4},{4,6},{6,8},{8,10},{10,12},{12,14},{14,16},{16,18},{18... | collective-permute-start | bytes 6152 | tf_op jit(solution)/shard_map/ppermute | solution.py:465
  32.0 0.6 copy-start.4
  32.0 1.0 copy-start
  58.4 28.6 %copy-start.6 = (bf16[512,512]{1,0:T(8,128)(2,1)S(1)}, bf16[512,512]{1,0:T(8,128)(2,1)}, u32[]{:S(2)}) copy-start(bf16[512,512]{1,0:T(8,128)(2,1)} %get-tuple-element.59) | copy-start | bytes 1572868
  58.4 29.8 %copy-start.5 = (bf16[512,512]{1,0:T(8,128)(2,1)S(1)}, bf16[512,512]{1,0:T(8,128)(2,1)}, u32[]{:S(2)}) copy-start(bf16[512,512]{1,0:T(8,128)(2,1)} %get-tuple-element.58) | copy-start | bytes 1572868
  71.1 3.9 %collective-permute-start.4 = (f32[1,2560]{1,0:T(1,128)}, f32[1,2560]{1,0:T(1,128)S(1)}, u32[]{:S(2)}, u32[]{:S(2)}) collective-permute-start(f32[1,2560]{1,0:T(1,128)} %get-tuple-element.69), channel_id=1, source_target_pairs={{0,2},{2,0},{4,6},{6,4},{8,10},{10,8},{12,14},{14,12},{16,18},{18,... | collective-permute-start | bytes 30728 | tf_op jit(solution)/shard_map/ppermute | solution.py:474
  75.7 3.7 %collective-permute-start.5 = (f32[1,2560]{1,0:T(1,128)S(1)}, f32[1,2560]{1,0:T(1,128)S(1)}, u32[]{:S(2)}, u32[]{:S(2)}) collective-permute-start(f32[1,2560]{1,0:T(1,128)S(1)} %add.24), channel_id=1, source_target_pairs={{0,4},{2,6},{4,0},{6,2},{8,12},{10,14},{12,8},{14,10},{16,20},{18,... | collective-permute-start | bytes 30728 | tf_op jit(solution)/shard_map/ppermute | solution.py:474
  79.5 4.3 %collective-permute-start.6 = (f32[1,2560]{1,0:T(1,128)S(1)}, f32[1,2560]{1,0:T(1,128)S(1)}, u32[]{:S(2)}, u32[]{:S(2)}) collective-permute-start(f32[1,2560]{1,0:T(1,128)S(1)} %add.25), channel_id=1, source_target_pairs={{0,8},{2,10},{4,12},{6,14},{8,0},{10,2},{12,4},{14,6},{16,24},{18,... | collective-permute-start | bytes 30728 | tf_op jit(solution)/shard_map/ppermute | solution.py:474
  83.8 5.7 %collective-permute-start.7 = (f32[1,2560]{1,0:T(1,128)S(1)}, f32[1,2560]{1,0:T(1,128)S(1)}, u32[]{:S(2)}, u32[]{:S(2)}) collective-permute-start(f32[1,2560]{1,0:T(1,128)S(1)} %add.26), channel_id=1, source_target_pairs={{0,16},{2,18},{4,20},{6,22},{8,24},{10,26},{12,28},{14,30},{16,0},... | collective-permute-start | bytes 30728 | tf_op jit(solution)/shard_map/ppermute | solution.py:474
  86.9 16.6 %collective-permute-start.3 = (bf16[512,512]{1,0:T(8,128)(2,1)S(1)}, bf16[512,512]{1,0:T(8,128)(2,1)S(1)}, u32[]{:S(2)}, u32[]{:S(2)}) collective-permute-start(bf16[512,512]{1,0:T(8,128)(2,1)S(1)} %copy-done.6), channel_id=1, source_target_pairs={{2,0},{4,2},{6,4},{8,6},{10,8},{12,10},{14,12},{16,14},{18,16},{20... | collective-permute-start | bytes 1572872 | tf_op jit(solution)/shard_map/ppermute | solution.py:465
  88.2 20.9 %collective-permute-start.2 = (bf16[512,512]{1,0:T(8,128)(2,1)S(1)}, bf16[512,512]{1,0:T(8,128)(2,1)S(1)}, u32[]{:S(2)}, u32[]{:S(2)}) collective-permute-start(bf16[512,512]{1,0:T(8,128)(2,1)S(1)} %copy-done.5), channel_id=1, source_target_pairs={{2,0},{4,2},{6,4},{8,6},{10,8},{12,10},{14,12},{16,14},{18,16},{20... | collective-permute-start | bytes 1572872 | tf_op jit(solution)/shard_map/ppermute | solution.py:465
  103.5 5.6 %copy-start.1 = (bf16[512,512]{1,0:T(8,128)(2,1)}, bf16[512,512]{1,0:T(8,128)(2,1)S(1)}, u32[]{:S(2)}) copy-start(bf16[512,512]{1,0:T(8,128)(2,1)S(1)} %collective-permute-done.3.refs_1_.refs_10_) | copy-start | bytes 1572868
  109.1 0.8 copy-start.2
